TPU v7x, 256 devices: a whole 4x4x8 slice. The times are simulated.
256 devices in a mesh: seq: 32 (over x, y, core), head: 8 (over z).
Axes of the slice: x: 4, y: 4, z: 8, core: 2. Of those that a mesh axis runs over, the one named last changes fastest.
Arguments:
- tokens: bfloat16 [32768, 2048], P('seq', 'head'), may hold values from -6 to 6
- seg_ids: int32 [32768], replicated, may hold values from 0 to 31, never falling along the last dimension, each value on 1 to 16384 neighbouring positions
- w_gate: bfloat16 [2048, 4096], P(None, 'head'), may hold values from -0.125 to 0.125
- w_x: bfloat16 [2048, 4096], P(None, 'head'), may hold values from -0.125 to 0.125
- w_bc: bfloat16 [2048, 256], replicated, may hold values from -0.125 to 0.125
- w_dt: bfloat16 [2048, 64], P(None, 'head'), may hold values from -0.125 to 0.125
- conv_x: float32 [4, 4096], P(None, 'head'), may hold values from -3 to 3
- conv_bc: float32 [4, 256], replicated, may hold values from -3 to 3
- conv_x_bias: float32 [4096], P('head'), may hold values from -3 to 3
- conv_bc_bias: float32 [256], replicated, may hold values from -3 to 3
- dt_bias: float32 [64], P('head'), may hold values from -4 to -1
- decay_rate: float32 [64], P('head'), may hold values from 0.0002 to 4
- skip_gain: float32 [64], P('head'), may hold values from 0.5 to 1.5
- norm_gain: float32 [4096], P('head'), may hold values from 0.5 to 1.5
- w_out: bfloat16 [4096, 2048], P('head'), may hold values from -0.125 to 0.125
Outputs:
- mixed: bfloat16 [32768, 2048], P('seq', 'head')
- end_state: float32 [32, 64, 64, 128], P('seq', 'head')
Inputs may be any that keep to these rules, and one draw needn't show every extreme that they name: `seg_ids`: prompt numbers never fall along the tokens; each prompt holds 1 to 16384 tokens, one of them exactly 16384.
All inputs are finite; a program needn't handle non-finite values.
Results may differ from a plain program's by a relative error of at most 0.0075.
Values may be sent and summed in bfloat16 or wider, within the bound.
A program may use at most 128 MiB of HBM per device.

v0:
```python
import jax
import jax.numpy as jnp
from jax import lax
from jax.sharding import PartitionSpec as P

GROUP = 256
INNER = 4096
EPSILON = 1e-05
HIGH = lax.Precision.HIGHEST


def shifted(x, axis, by):
    devices = lax.axis_size(axis)
    pairs = [(i, i + by) for i in range(devices) if 0 <= i + by < devices]
    return lax.ppermute(x, axis, pairs)


def carried_in(part, axis, combine, identity):
    place = lax.axis_index(axis)
    gathered = jax.tree.map(lambda a: lax.all_gather(a, axis), part)
    state = jax.tree.map(lambda a, e: jnp.zeros_like(a) + jnp.asarray(e, a.dtype), part, identity)

    def one(hop, state):
        return combine(
            state, jax.tree.map(lambda a: lax.dynamic_index_in_dim(a, hop, 0, False), gathered)
        )

    return lax.fori_loop(0, place, one, state)


def conv_block(projected, edge_rows, weights, offsets, idents, earlier):
    rows_here = projected.shape[0]
    lag_count = edge_rows.shape[0]
    joined = jnp.concatenate([edge_rows, projected], 0).astype(jnp.float32)
    joined_ids = jnp.concatenate([earlier, idents], 0)
    result = joined[lag_count:] * weights[0]
    for shift_by in range(1, lag_count + 1):
        window = joined[lag_count - shift_by : lag_count - shift_by + rows_here]
        matches = joined_ids[lag_count - shift_by : lag_count - shift_by + rows_here] == idents
        result = result + jnp.where(matches[:, None], window, 0.0) * weights[shift_by]
    return result + offsets


def combine(earlier, later):
    return (earlier[0] * later[0], later[0][:, None, None] * earlier[1] + later[1])


def shards(
    tokens,
    seg_ids,
    w_gate,
    w_x,
    w_bc,
    w_dt,
    conv_x,
    conv_bc,
    conv_x_bias,
    conv_bc_bias,
    dt_bias,
    decay_rate,
    skip_gain,
    norm_gain,
    w_out,
):
    rows_here = tokens.shape[0]
    heads_here = w_dt.shape[1]
    inner_here = w_x.shape[1]
    head_width = inner_here // heads_here
    state_width = w_bc.shape[1] // 2
    lag_count = conv_x.shape[0] - 1
    device = lax.axis_index("seq")
    first_row = device * rows_here
    piece = lax.all_gather(tokens, "head", axis=1, tiled=True)

    def partial_product(matrix):
        return jnp.dot(piece, matrix, preferred_element_type=jnp.float32)

    gate_full = partial_product(w_gate)
    x_sum = partial_product(w_x)
    bc_sum = partial_product(w_bc)
    dt_raw = partial_product(w_dt)
    x_pre = x_sum.astype(jnp.bfloat16)
    bc_pre = bc_sum.astype(jnp.bfloat16)
    idents = lax.dynamic_slice_in_dim(seg_ids, first_row, rows_here)
    earlier = lax.dynamic_slice_in_dim(seg_ids, jnp.maximum(first_row - lag_count, 0), lag_count)
    earlier = jnp.where(device > 0, earlier, -1)
    edge_x, edge_bc = shifted(
        (x_pre[rows_here - lag_count :], bc_pre[rows_here - lag_count :]), "seq", 1
    )
    x_conv = jax.nn.silu(conv_block(x_pre, edge_x, conv_x, conv_x_bias, idents, earlier)).astype(
        jnp.bfloat16
    )
    bc_conv = jax.nn.silu(
        conv_block(bc_pre, edge_bc, conv_bc, conv_bc_bias, idents, earlier)
    ).astype(jnp.bfloat16)
    steps_dt = jax.nn.softplus(dt_raw + dt_bias)
    log_decay = -steps_dt * decay_rate
    x_float = x_conv.astype(jnp.float32).reshape(rows_here, heads_here, head_width)
    x_scaled = x_float * steps_dt[:, :, None]
    count = rows_here // GROUP
    group_x = x_scaled.reshape(count, GROUP, heads_here, head_width)
    group_b = bc_conv[:, :state_width].astype(jnp.float32).reshape(count, GROUP, state_width)
    group_c = bc_conv[:, state_width:].astype(jnp.float32).reshape(count, GROUP, state_width)
    group_ids = idents.reshape(count, GROUP)
    cumul = jnp.cumsum(log_decay.reshape(count, GROUP, heads_here), axis=1)
    cumul_heads = jnp.transpose(cumul, (0, 2, 1))
    places = jnp.arange(GROUP)
    causal = places[None, :] <= places[:, None]
    linked = causal[None] & (group_ids[:, :, None] == group_ids[:, None, :])
    gaps = cumul_heads[:, :, :, None] - cumul_heads[:, :, None, :]
    link_heads = linked[:, None, :, :]
    decays = jnp.where(link_heads, jnp.exp(jnp.where(link_heads, gaps, 0.0)), 0.0)
    scores = jnp.einsum("ctn,csn->cts", group_c, group_b, precision=HIGH)
    within = jnp.einsum("chts,cshp->cthp", decays * scores[:, None, :, :], group_x, precision=HIGH)
    last_ids = group_ids[:, -1]
    tails = jnp.where(
        (group_ids == last_ids[:, None])[:, :, None], jnp.exp(cumul[:, -1:, :] - cumul), 0.0
    )
    group_states = jnp.einsum(
        "cshp,csn->chpn", group_x * tails[:, :, :, None], group_b, precision=HIGH
    )
    prior_ids = jnp.concatenate([earlier[-1:], last_ids[:-1]], 0)
    passing = jnp.where((last_ids == prior_ids)[:, None], jnp.exp(cumul[:, -1, :]), 0.0)
    local_list = []
    gain_list = []
    running_state = jnp.zeros((heads_here, head_width, state_width), jnp.float32)
    running_gain = jnp.ones((heads_here,), jnp.float32)
    for group_no in range(count):
        local_list.append(running_state)
        gain_list.append(running_gain)
        running_state = passing[group_no][:, None, None] * running_state + group_states[group_no]
        running_gain = passing[group_no] * running_gain
    identity = (jnp.ones_like(running_gain), jnp.zeros_like(running_state))
    prefix_gain, incoming = carried_in((running_gain, running_state), "seq", combine, identity)
    entering = jnp.stack(gain_list, 0)[:, :, None, None] * incoming[None] + jnp.stack(local_list, 0)
    enter_weight = jnp.where((group_ids == prior_ids[:, None])[:, :, None], jnp.exp(cumul), 0.0)
    carried = (
        jnp.einsum("ctn,chpn->cthp", group_c, entering, precision=HIGH)
        * enter_weight[:, :, :, None]
    )
    end_state = (running_gain[:, None, None] * incoming + running_state)[None]
    ssd_out = (within + carried).reshape(rows_here, heads_here, head_width) + skip_gain[
        None, :, None
    ] * x_float
    gated = ssd_out.reshape(rows_here, inner_here) * jax.nn.silu(gate_full)
    square_total = lax.psum(jnp.sum(gated * gated, axis=1), "head")
    mean_square = (square_total / INNER)[:, None]
    hidden = (gated * lax.rsqrt(mean_square + EPSILON) * norm_gain).astype(jnp.bfloat16)
    partial_out = jnp.dot(hidden, w_out, preferred_element_type=jnp.float32)
    mixed = lax.psum_scatter(partial_out, "head", scatter_dimension=1, tiled=True).astype(
        jnp.bfloat16
    )
    return (mixed, end_state)


def solution(mesh):
    return jax.shard_map(
        shards,
        mesh=mesh,
        in_specs=(
            P("seq", "head"),
            P(),
            P(None, "head"),
            P(None, "head"),
            P(),
            P(None, "head"),
            P(None, "head"),
            P(),
            P("head"),
            P(),
            P("head"),
            P("head"),
            P("head"),
            P("head"),
            P("head", None),
        ),
        out_specs=(P("seq", "head"), P("seq", "head", None, None)),
        check_vma=False,
    )
```

profile of v0, /device:TPU:1, one launch (start us, length us, event | category | flops | bytes accessed | tf_op | source)
XLA Modules:
  0.0 347.8 jit_solution(15108138510818791325)
XLA Ops:
  11.1 0.8 fusion.53
  12.1 0.8 fusion.61
  12.9 0.9 fusion.59
  13.8 58.4 %all-gather.4.cloned.1.call-done = bf16[1024,2048]{1,0:T(8,128)(2,1)} async-done(((bf16[1024,256]{1,0:T(8,128)(2,1)}), bf16[1024,2048]{1,0:T(8,128)(2,1)}) %all-gather.4.cloned.1.call-update) | async-done | bytes 4194320 | tf_op jit(solution)/shard_map/all_gather | solution.py:73
  72.3 3.9 %convolution_convert_fusion.1 = bf16[1024,256]{1,0:T(8,128)(2,1)S(1)} fusion(bf16[1024,2048]{1,0:T(8,128)(2,1)} %all-gather.4.cloned.1.call-done, bf16[2048,256]{1,0:T(8,128)(2,1)} %param.21), kind=kOutput, calls=%fused_computation.33 | convolution fusion | flops 1074003968 | bytes 5767168 | tf_op jit(solution)/shard_map/dot_general | solution.py:76
  76.2 7.4 %collective-permute-start.1 = (bf16[3,256]{1,0:T(4,128)(2,1)S(1)}, bf16[3,256]{1,0:T(4,128)(2,1)S(1)}, u32[]{:S(2)}, u32[]{:S(2)}) collective-permute-start(bf16[3,256]{1,0:T(4,128)(2,1)S(1)} %slice.175), channel_id=1, source_target_pairs={{0,8},{8,16},{16,24},{24,32},{32,40},{40,48},{48,56},{56,64},{64,7... | collective-permute-start | bytes 4616 | tf_op jit(solution)/shard_map/ppermute | solution.py:15
  83.6 1.2 negate_multiply_fusion
  84.8 2.3 reduce-window.6
  87.7 5.2 %convolution_convert_fusion = bf16[1024,512]{1,0:T(8,128)(2,1)S(1)} fusion(bf16[1024,2048]{1,0:T(8,128)(2,1)} %all-gather.4.cloned.1.call-done, bf16[2048,512]{1,0:T(8,128)(2,1)} %param.20), kind=kOutput, calls=%fused_computation.32 | convolution fusion | flops 2148007936 | bytes 7340032 | tf_op jit(solution)/shard_map/dot_general | solution.py:76
  93.0 1.9 collective-permute-start
  95.1 1.3 multiply_convert_fusion.3
  97.5 3.1 fusion.37
  100.7 2.9 copy.64
  103.6 3.2 reshape.162
  106.8 3.8 %broadcast_multiply_fusion = (f32[4,256,8,64]{1,0,3,2:T(4,128)S(1)}, f32[4,256,8,64]{1,0,3,2:T(4,128)}) fusion(f32[4,256,8]{1,0,2:T(4,128)S(1)} %copy.69, f32[4,256,8,64]{1,0,3,2:T(4,128)} %reshape.162, f32[4,256,8]{1,0,2:T(4,128)S(1)} %copy.65), kind=kLoop, calls=%fused_computation.57 | loop fusion | flops 1048576 | bytes 6356992 | tf_op jit(solution)/shard_map/mul | solution.py:120
  110.6 1.3 fusion.18
  111.9 1.1 multiply_add_fusion
  113.5 22.6 %all-gather = f32[32,1,8]{2,1,0:T(1,128)S(1)} all-gather(f32[1,1,8]{2,1,0:T(1,128)S(1)} %get-tuple-element.93), channel_id=1, replica_groups=mesh['seq'=32,'head'=8] {'seq'}, dimensions={0}, use_global_device_ids=true | all-gather | bytes 1056 | tf_op jit(solution)/shard_map/all_gather | solution.py:20
  136.3 1.2 fusion.63
  137.5 12.0 %fusion = f32[4,8,64,256]{3,2,1,0:T(8,128)} fusion(f32[4,256,256]{2,1,0:T(8,128)S(1)} %fusion.63, f32[4,8,256]{2,1,0:T(8,128)S(1)} %add_bitcast_fusion.1, pred[4,256,256]{2,1,0:T(8,128)(4,1)S(1)} %compare_and_fusion, f32[4,256,8,64]{1,0,3,2:T(4,128)} %get-tuple-element.69), kind=kOutput, calls=%fused_computation.2 | convolution fusion | flops 1619001344 | bytes 5537792 | tf_op jit(solution)/shard_map/chts,cshp->cthp/dot_general | solution.py:114
  149.6 20.0 %all-gather.6.cloned.1.call-done = f32[32,8,64,128]{3,2,1,0:T(8,128)} async-done(((f32[1,8,64,128]{3,2,1,0:T(8,128)}), f32[32,8,64,128]{3,2,1,0:T(8,128)}) %all-gather.6.cloned.1.call-update) | async-done | bytes 8388624 | tf_op jit(solution)/shard_map/all_gather | solution.py:20
  169.6 1.1 while.12
  169.6 1.1 bitcast_add_fusion.7
  170.7 4.3 %bitcast_add_fusion.1 = f32[4,256,8,64]{1,3,2,0:T(8,128)} fusion(f32[4,8,64,256]{3,2,1,0:T(8,128)} %fusion, bf16[4,256,128,1]{2,1,3,0:T(8,128)(2,1)} %bitcast.114, f32[1,8,64,128]{3,2,1,0:T(8,128)} %get-tuple-element.60, f32[1,8,64,128]{3,2,1,0:T(8,128)} %get-tuple-element.61, f32[1,8,64,128]{3,2,1,0:T(8,128)} %get-tuple-element.62, ...), kind=kOutput, calls=%fused_computation.24 | convolution fusion | flops 807665664 | bytes 5537936 | tf_op jit(solution)/shard_map/ctn,chpn->cthp/dot_general | solution.py:138
  175.0 3.8 %copy.78 = f32[4,256,8,64]{3,2,1,0:T(8,128)} copy(f32[4,256,8,64]{1,3,2,0:T(8,128)} %bitcast_add_fusion.1) | data formatting | bytes 4194304 | tf_op jit(solution)/shard_map/reshape | solution.py:142
  178.8 4.8 %reshape.173 = f32[1024,512]{1,0:T(8,128)} reshape(f32[4,256,8,64]{3,2,1,0:T(8,128)} %copy.78) | data formatting | bytes 4194304 | tf_op jit(solution)/shard_map/reshape | solution.py:142
  183.6 8.1 %multiply_reduce_fusion = (f32[1024]{0:T(1024)S(1)}, f32[1024,512]{1,0:T(8,128)}) fusion(f32[1024,512]{1,0:T(8,128)} %reshape.173, f32[1024,512]{1,0:T(8,128)} %fusion.37, f32[512]{0:T(512)S(1)} %mul.359, bf16[1024,2048]{1,0:T(8,128)(2,1)} %all-gather.4.cloned.1.call-done, bf16[2048,512]{1,0:T(8,128)(2,1)} %param.19), kind=kOutput, calls=%fused_computation.29 | convolution fusion | flops 2152201216 | bytes 12589056 | tf_op jit(solution)/shard_map/dot_general | solution.py:76
  191.7 13.7 %psum.7 = f32[1024]{0:T(1024)S(1)} all-reduce(f32[1024]{0:T(1024)S(1)} %get-tuple-element.57), channel_id=1, replica_groups=mesh['seq'=32,'head'=8] {'head'}, use_global_device_ids=true, to_apply=%region_5.6 | all-reduce | flops 1024 | bytes 8192 | tf_op jit(solution)/shard_map/psum | solution.py:146
  205.4 7.2 %fusion.21 = f32[1024,2048]{1,0:T(8,128)} fusion(bf16[512,2048]{1,0:T(8,128)(2,1)S(1)} %copy-done, f32[1024,512]{1,0:T(8,128)} %get-tuple-element.58, f32[512]{0:T(512)S(1)} %copy-done.3, f32[1024]{0:T(1024)S(1)} %add_rsqrt_fusion), kind=kOutput, calls=%fused_computation.36 | convolution fusion | flops 2149056512 | bytes 12589056 | tf_op jit(solution)/shard_map/dot_general | solution.py:149
  212.7 0.9 fusion.42
  213.5 125.7 %reduce-scatter.2.cloned.1.call-done = f32[1024,256]{1,0:T(8,128)} async-done(((f32[1024,2048]{1,0:T(8,128)}), f32[1024,256]{1,0:T(8,128)}) %reduce-scatter.2.cloned.1.call-update) | async-done | bytes 1048592 | tf_op jit(solution)/shard_map/reduce_scatter | solution.py:150
  339.2 2.1 convert_element_type.37
  (64 shorter events, 6.6 us)
Async XLA Ops:
  7.2 198.2 %copy-start = (bf16[512,2048]{1,0:T(8,128)(2,1)S(1)}, bf16[512,2048]{1,0:T(8,128)(2,1)}, u32[]{:S(2)}) copy-start(bf16[512,2048]{1,0:T(8,128)(2,1)} %param.31) | copy-start | bytes 6291460
  7.2 65.1 %all-gather.4.cloned.1.call-start = ((), (), s32[]{:S(2)}) async-start(), calls=%async_computation.1 | async-start | bytes 4718592 | tf_op jit(solution)/shard_map/all_gather | solution.py:73
  7.9 161.6 %all-gather.6.cloned.1.call-start = ((), (), s32[]{:S(2)}) async-start(), calls=%async_computation.2 | async-start | bytes 8650752 | tf_op jit(solution)/shard_map/all_gather | solution.py:20
  13.8 69.8 %copy-start.2 = (bf16[2048,8]{0,1:T(8,128)(2,1)S(1)}, bf16[2048,8]{0,1:T(8,128)(2,1)}, u32[]{:S(2)}) copy-start(bf16[2048,8]{0,1:T(8,128)(2,1)} %param.22) | copy-start | bytes 98308
  13.8 69.8 %copy-start.5 = (f32[8]{0:T(128)S(1)}, f32[8]{0:T(128)}, u32[]{:S(2)}) copy-start(f32[8]{0:T(128)} %param.28) | copy-start | bytes 100
  13.8 69.8 %copy-start.6 = (f32[8]{0:T(128)S(1)}, f32[8]{0:T(128)}, u32[]{:S(2)}) copy-start(f32[8]{0:T(128)} %param.27) | copy-start | bytes 100
  72.3 11.3 %copy-start.1 = (bf16[1024,2048]{1,0:T(8,128)(2,1)S(1)}, bf16[1024,2048]{1,0:T(8,128)(2,1)}, u32[]{:S(2)}) copy-start(bf16[1024,2048]{1,0:T(8,128)(2,1)} %all-gather.4.cloned.1.call-done) | copy-start | bytes 12582916
  76.2 18.8 %collective-permute-start.1 = (bf16[3,256]{1,0:T(4,128)(2,1)S(1)}, bf16[3,256]{1,0:T(4,128)(2,1)S(1)}, u32[]{:S(2)}, u32[]{:S(2)}) collective-permute-start(bf16[3,256]{1,0:T(4,128)(2,1)S(1)} %slice.175), channel_id=1, source_target_pairs={{0,8},{8,16},{16,24},{24,32},{32,40},{40,48},{48,56},{56,64},{64,7... | collective-permute-start | bytes 4616 | tf_op jit(solution)/shard_map/ppermute | solution.py:15
  87.7 7.3 %copy-start.7 = (f32[256]{0:T(256)S(1)}, f32[256]{0:T(256)}, u32[]{:S(2)}) copy-start(f32[256]{0:T(256)} %param.26) | copy-start | bytes 3076
  93.0 4.2 %collective-permute-start = (bf16[3,512]{1,0:T(4,128)(2,1)S(1)}, bf16[3,512]{1,0:T(4,128)(2,1)S(1)}, u32[]{:S(2)}, u32[]{:S(2)}) collective-permute-start(bf16[3,512]{1,0:T(4,128)(2,1)S(1)} %slice.164), channel_id=1, source_target_pairs={{0,8},{8,16},{16,24},{24,32},{32,40},{40,48},{48,56},{56,64},{64,7... | collective-permute-start | bytes 9224 | tf_op jit(solution)/shard_map/ppermute | solution.py:15
  96.4 1.1 copy-start.4
  110.6 2.4 copy-start.8
  112.9 226.3 %reduce-scatter.2.cloned.1.call-start = ((), (), s32[]{:S(2)}) async-start(), calls=%async_computation.3 | async-start | bytes 9437184 | tf_op jit(solution)/shard_map/reduce_scatter | solution.py:150
  183.6 21.8 %copy-start.3 = (f32[512]{0:T(512)S(1)}, f32[512]{0:T(512)}, u32[]{:S(2)}) copy-start(f32[512]{0:T(512)} %param.30) | copy-start | bytes 6148
Sparse Core Ops, SparseCore 0:
  9.7 62.5 all-gather.3
  113.1 56.4 all-gather.5
  212.8 126.4 reduce-scatter.1
where the time goes:
time: 349 us; the launch traced here: 348 us
  waiting for transfers between devices  205 us (59%)
  matrix products  44.5 us (13%)
  blocking collectives  36.3 us (10%)
  local copies, waits for them, and re-layouts  19.5 us (6%)
  other arithmetic  19.2 us (6%)
  between operations  14.1 us (4%)
  starting transfers between devices  9.41 us (3%)
    reduce_scatter x1, waiting for transfers between devices, shards(): lax.psum_scatter(partial_out, 'head', scatter_dimension=1, tiled=True)  126 us
    all_gather x1, waiting for transfers between devices, shards(): piece = lax.all_gather(tokens, 'head', axis=1, tiled=True)  58.4 us
    all_gather x1, blocking collectives, carried_in(): gathered = jax.tree.map(lambda a: lax.all_gather(a, axis), part)  22.6 us
    all_gather x1, waiting for transfers between devices, carried_in(): gathered = jax.tree.map(lambda a: lax.all_gather(a, axis), part)  20 us
    dot_general x4, matrix products, partial_product(): return jnp.dot(piece, matrix, preferred_element_type=jnp.float32)  18.4 us
    psum x1, blocking collectives, shards(): square_total = lax.psum(jnp.sum(gated * gated, axis=1), 'head')  13.7 us
    dot_general x1, matrix products, shards(): jnp.einsum('chts,cshp->cthp', decays * scores[:, None, :, :], group_x, pr...  12 us
    ppermute x2, starting transfers between devices, shifted(): return lax.ppermute(x, axis, pairs)  9.29 us
  transfers between devices with their start and end apart: 5, of which 3 were waited for; matrix products, arithmetic and copies ran while one was open for 9% of the time, Pallas kernels for 0%

commit v1 on v0

--- a/solution.py
+++ b/solution.py
@@ -7,6 +7,12 @@
 INNER = 4096
 EPSILON = 1e-05
 HIGH = lax.Precision.HIGHEST
+
+
+def _pack_strings(u_in):
+    return jnp.concatenate(
+        lax.all_to_all(jnp.stack([u_in] * lax.psum(1, "head")), "head", 0, 0), axis=1
+    )
 
 
 def shifted(x, axis, by):
@@ -70,7 +76,7 @@
     lag_count = conv_x.shape[0] - 1
     device = lax.axis_index("seq")
     first_row = device * rows_here
-    piece = lax.all_gather(tokens, "head", axis=1, tiled=True)
+    piece = _pack_strings(tokens)
 
     def partial_product(matrix):
         return jnp.dot(piece, matrix, preferred_element_type=jnp.float32)

time: 349 us -> 390 us (1.12)
  waiting for transfers between devices: 205 us -> 236 us
  starting transfers between devices: 9.41 us -> 14.7 us
    all_to_all x0 -> x1, waiting for transfers between devices: none -> 92.6 us  [_pack_strings(): lax.all_to_all(jnp.stack([u_in] * lax.psum(1, 'head')), 'head', 0, 0)]
    all_gather x1 -> x0, waiting for transfers between devices: 58.4 us -> none  [shards(): piece = lax.all_gather(tokens, 'head', axis=1, tiled=True)]
    all_to_all x0 -> x1, starting transfers between devices: none -> 9.13 us  [_pack_strings(): lax.all_to_all(jnp.stack([u_in] * lax.psum(1, 'head')), 'head', 0, 0)]
  transfers between devices with their start and end apart: 5 -> 5, of which waited for: 3 -> 3; matrix products, arithmetic and copies ran while one was open for 9% -> 8% of each run, Pallas kernels for 0% -> 0%
where the time goes in v1:
time: 390 us; the launch traced here: 388 us
  waiting for transfers between devices  236 us (61%)
  matrix products  46.1 us (12%)
  blocking collectives  36.3 us (9%)
  local copies, waits for them, and re-layouts  21.7 us (6%)
  other arithmetic  19.2 us (5%)
  starting transfers between devices  14.7 us (4%)
  between operations  14.3 us (4%)
    reduce_scatter x1, waiting for transfers between devices, shards(): lax.psum_scatter(partial_out, 'head', scatter_dimension=1, tiled=True)  126 us
    all_to_all x1, waiting for transfers between devices, _pack_strings(): lax.all_to_all(jnp.stack([u_in] * lax.psum(1, 'head')), 'head', 0, 0)  92.6 us
    all_gather x1, blocking collectives, carried_in(): gathered = jax.tree.map(lambda a: lax.all_gather(a, axis), part)  22.6 us
    dot_general x4, matrix products, partial_product(): return jnp.dot(piece, matrix, preferred_element_type=jnp.float32)  20.1 us
    all_gather x1, waiting for transfers between devices, carried_in(): gathered = jax.tree.map(lambda a: lax.all_gather(a, axis), part)  17.7 us
    psum x1, blocking collectives, shards(): square_total = lax.psum(jnp.sum(gated * gated, axis=1), 'head')  13.7 us
    dot_general x1, matrix products, shards(): jnp.einsum('chts,cshp->cthp', decays * scores[:, None, :, :], group_x, pr...  12 us
    all_to_all x1, starting transfers between devices, _pack_strings(): lax.all_to_all(jnp.stack([u_in] * lax.psum(1, 'head')), 'head', 0, 0)  9.13 us
  transfers between devices with their start and end apart: 5, of which 3 were waited for; matrix products, arithmetic and copies ran while one was open for 8% of the time, Pallas kernels for 0%

profile of v1, /device:TPU:1, one launch (start us, length us, event | category | flops | bytes accessed | tf_op | source)
XLA Modules:
  0.0 388.4 jit_solution(1629076857514512629)
XLA Ops:
  7.2 1.4 copy.67
  8.6 2.5 stack.6
  11.1 9.1 %all-to-all-start = ((bf16[8,1024,256]{1,2,0:T(8,128)(2,1)}), bf16[8,1024,256]{1,2,0:T(8,128)(2,1)}, u32[]{:S(2)}, u32[]{:S(2)}) async-start(bf16[8,1024,256]{1,2,0:T(8,128)(2,1)} %stack.6), calls=%async_computation | async-start | bytes 8388608 | tf_op jit(solution)/shard_map/all_to_all | solution.py:14
  24.4 92.6 %all-to-all-done = bf16[8,1024,256]{1,2,0:T(8,128)(2,1)} async-done(((bf16[8,1024,256]{1,2,0:T(8,128)(2,1)}), bf16[8,1024,256]{1,2,0:T(8,128)(2,1)}, u32[]{:S(2)}, u32[]{:S(2)}) %all-to-all-start) | async-done | bytes 4194336 | tf_op jit(solution)/shard_map/all_to_all | solution.py:14
  117.1 3.8 convolution_convert_fusion.1
  120.9 3.6 collective-permute-start.1
  124.5 2.9 negate_multiply_fusion
  127.4 2.3 reduce-window.6
  130.1 5.2 %convolution_convert_fusion = bf16[1024,512]{1,0:T(8,128)(2,1)S(1)} fusion(bf16[1024,2048]{0,1:T(8,128)(2,1)} %bitcast.3, bf16[2048,512]{1,0:T(8,128)(2,1)} %param.20), kind=kOutput, calls=%fused_computation.32 | convolution fusion | flops 2148007936 | bytes 7340032 | tf_op jit(solution)/shard_map/dot_general | solution.py:82
  135.6 1.9 collective-permute-start
  137.7 1.3 multiply_convert_fusion.3
  140.1 3.1 fusion.37
  143.3 2.9 copy.68
  146.2 3.2 reshape.172
  149.4 3.8 broadcast_multiply_fusion
  153.2 1.3 fusion.18
  154.5 1.1 multiply_add_fusion
  156.1 22.6 %all-gather = f32[32,1,8]{2,1,0:T(1,128)S(1)} all-gather(f32[1,1,8]{2,1,0:T(1,128)S(1)} %get-tuple-element.93), channel_id=1, replica_groups=mesh['seq'=32,'head'=8] {'seq'}, dimensions={0}, use_global_device_ids=true | all-gather | bytes 1056 | tf_op jit(solution)/shard_map/all_gather | solution.py:26
  178.8 1.2 fusion.63
  180.1 12.0 %fusion = f32[4,8,64,256]{3,2,1,0:T(8,128)} fusion(f32[4,256,256]{2,1,0:T(8,128)S(1)} %fusion.63, f32[4,8,256]{2,1,0:T(8,128)S(1)} %add_bitcast_fusion.1, pred[4,256,256]{2,1,0:T(8,128)(4,1)S(1)} %compare_and_fusion, f32[4,256,8,64]{1,0,3,2:T(4,128)} %get-tuple-element.69), kind=kOutput, calls=%fused_computation.2 | convolution fusion | flops 1619001344 | bytes 5537792 | tf_op jit(solution)/shard_map/chts,cshp->cthp/dot_general | solution.py:120
  192.1 17.7 %all-gather.3.cloned.1.call-done = f32[32,8,64,128]{3,2,1,0:T(8,128)} async-done(((f32[1,8,64,128]{3,2,1,0:T(8,128)}), f32[32,8,64,128]{3,2,1,0:T(8,128)}) %all-gather.3.cloned.1.call-update) | async-done | bytes 8388624 | tf_op jit(solution)/shard_map/all_gather | solution.py:26
  209.8 1.1 while.12
  209.9 1.1 bitcast_add_fusion.7
  210.9 4.3 %bitcast_add_fusion.1 = f32[4,256,8,64]{1,3,2,0:T(8,128)} fusion(f32[4,8,64,256]{3,2,1,0:T(8,128)} %fusion, bf16[4,256,128,1]{2,1,3,0:T(8,128)(2,1)} %bitcast.117, f32[1,8,64,128]{3,2,1,0:T(8,128)} %get-tuple-element.60, f32[1,8,64,128]{3,2,1,0:T(8,128)} %get-tuple-element.61, f32[1,8,64,128]{3,2,1,0:T(8,128)} %get-tuple-element.62, ...), kind=kOutput, calls=%fused_computation.24 | convolution fusion | flops 807665664 | bytes 5537936 | tf_op jit(solution)/shard_map/ctn,chpn->cthp/dot_general | solution.py:144
  215.3 3.8 copy.82
  219.1 4.8 %reshape.183 = f32[1024,512]{1,0:T(8,128)} reshape(f32[4,256,8,64]{3,2,1,0:T(8,128)} %copy.82) | data formatting | bytes 4194304 | tf_op jit(solution)/shard_map/reshape | solution.py:148
  223.9 8.1 %multiply_reduce_fusion = (f32[1024]{0:T(1024)S(1)}, f32[1024,512]{1,0:T(8,128)}) fusion(f32[1024,512]{1,0:T(8,128)} %reshape.183, f32[1024,512]{1,0:T(8,128)} %fusion.37, f32[512]{0:T(512)S(1)} %mul.359, bf16[1024,2048]{0,1:T(8,128)(2,1)} %bitcast.3, bf16[2048,512]{1,0:T(8,128)(2,1)} %param.19), kind=kOutput, calls=%fused_computation.29 | convolution fusion | flops 2152201216 | bytes 12589056 | tf_op jit(solution)/shard_map/dot_general | solution.py:82
  232.0 13.7 %psum.7 = f32[1024]{0:T(1024)S(1)} all-reduce(f32[1024]{0:T(1024)S(1)} %get-tuple-element.57), channel_id=1, replica_groups=mesh['seq'=32,'head'=8] {'head'}, use_global_device_ids=true, to_apply=%region_5.6 | all-reduce | flops 1024 | bytes 8192 | tf_op jit(solution)/shard_map/psum | solution.py:152
  245.7 7.2 %fusion.21 = f32[1024,2048]{1,0:T(8,128)} fusion(bf16[512,2048]{1,0:T(8,128)(2,1)S(1)} %copy-done, f32[1024,512]{1,0:T(8,128)} %get-tuple-element.58, f32[512]{0:T(512)S(1)} %copy-done.2, f32[1024]{0:T(1024)S(1)} %add_rsqrt_fusion), kind=kOutput, calls=%fused_computation.36 | convolution fusion | flops 2149056512 | bytes 12589056 | tf_op jit(solution)/shard_map/dot_general | solution.py:155
  253.0 0.9 fusion.42
  253.8 125.7 %reduce-scatter.2.cloned.1.call-done = f32[1024,256]{1,0:T(8,128)} async-done(((f32[1024,2048]{1,0:T(8,128)}), f32[1024,256]{1,0:T(8,128)}) %reduce-scatter.2.cloned.1.call-update) | async-done | bytes 1048592 | tf_op jit(solution)/shard_map/reduce_scatter | solution.py:156
  379.5 2.1 convert_element_type.37
  (67 shorter events, 6.7 us)
Async XLA Ops:
  7.2 238.5 %copy-start = (bf16[512,2048]{1,0:T(8,128)(2,1)S(1)}, bf16[512,2048]{1,0:T(8,128)(2,1)}, u32[]{:S(2)}) copy-start(bf16[512,2048]{1,0:T(8,128)(2,1)} %param.31) | copy-start | bytes 6291460
  11.1 13.3 %copy-start.4 = (f32[4,256]{1,0:T(4,128)S(1)}, f32[4,256]{1,0:T(4,128)}, u32[]{:S(2)}) copy-start(f32[4,256]{1,0:T(4,128)} %param.24) | copy-start | bytes 12292
  11.1 13.3 %copy-start.3 = (f32[4,512]{1,0:T(4,128)S(1)}, f32[4,512]{1,0:T(4,128)}, u32[]{:S(2)}) copy-start(f32[4,512]{1,0:T(4,128)} %param.23) | copy-start | bytes 24580
  11.1 106.0 %all-to-all-start = ((bf16[8,1024,256]{1,2,0:T(8,128)(2,1)}), bf16[8,1024,256]{1,2,0:T(8,128)(2,1)}, u32[]{:S(2)}, u32[]{:S(2)}) async-start(bf16[8,1024,256]{1,2,0:T(8,128)(2,1)} %stack.6), calls=%async_computation | async-start | bytes 8388608 | tf_op jit(solution)/shard_map/all_to_all | solution.py:14
  20.2 189.6 %all-gather.3.cloned.1.call-start = ((), (), s32[]{:S(2)}) async-start(), calls=%async_computation.2 | async-start | bytes 8650752 | tf_op jit(solution)/shard_map/all_gather | solution.py:26
  117.0 7.4 %copy-start.1 = (bf16[2048,8]{0,1:T(8,128)(2,1)S(1)}, bf16[2048,8]{0,1:T(8,128)(2,1)}, u32[]{:S(2)}) copy-start(bf16[2048,8]{0,1:T(8,128)(2,1)} %param.22) | copy-start | bytes 98308
  117.0 7.4 %copy-start.6 = (f32[8]{0:T(128)S(1)}, f32[8]{0:T(128)}, u32[]{:S(2)}) copy-start(f32[8]{0:T(128)} %param.28) | copy-start | bytes 100
  117.1 7.5 %copy-start.7 = (f32[8]{0:T(128)S(1)}, f32[8]{0:T(128)}, u32[]{:S(2)}) copy-start(f32[8]{0:T(128)} %param.27) | copy-start | bytes 100
  120.9 16.6 %collective-permute-start.1 = (bf16[3,256]{1,0:T(4,128)(2,1)S(1)}, bf16[3,256]{1,0:T(4,128)(2,1)S(1)}, u32[]{:S(2)}, u32[]{:S(2)}) collective-permute-start(bf16[3,256]{1,0:T(4,128)(2,1)S(1)} %slice.175), channel_id=1, source_target_pairs={{0,8},{8,16},{16,24},{24,32},{32,40},{40,48},{48,56},{56,64},{64,7... | collective-permute-start | bytes 4616 | tf_op jit(solution)/shard_map/ppermute | solution.py:21
  130.1 7.5 %copy-start.8 = (f32[256]{0:T(256)S(1)}, f32[256]{0:T(256)}, u32[]{:S(2)}) copy-start(f32[256]{0:T(256)} %param.26) | copy-start | bytes 3076
  135.6 4.2 %collective-permute-start = (bf16[3,512]{1,0:T(4,128)(2,1)S(1)}, bf16[3,512]{1,0:T(4,128)(2,1)S(1)}, u32[]{:S(2)}, u32[]{:S(2)}) collective-permute-start(bf16[3,512]{1,0:T(4,128)(2,1)S(1)} %slice.164), channel_id=1, source_target_pairs={{0,8},{8,16},{16,24},{24,32},{32,40},{40,48},{48,56},{56,64},{64,7... | collective-permute-start | bytes 9224 | tf_op jit(solution)/shard_map/ppermute | solution.py:21
  139.0 1.1 copy-start.5
  153.2 2.4 copy-start.9
  155.5 224.0 %reduce-scatter.2.cloned.1.call-start = ((), (), s32[]{:S(2)}) async-start(), calls=%async_computation.3 | async-start | bytes 9437184 | tf_op jit(solution)/shard_map/reduce_scatter | solution.py:156
  223.9 21.8 %copy-start.2 = (f32[512]{0:T(512)S(1)}, f32[512]{0:T(512)}, u32[]{:S(2)}) copy-start(f32[512]{0:T(512)} %param.30) | copy-start | bytes 6148
Sparse Core Ops, SparseCore 0:
  155.7 54.1 all-gather.2
  253.1 126.4 reduce-scatter.1
